TPU v7x, 128 devices: a whole 4x4x4 slice. The times are simulated.
128 devices in a mesh: row: 16 (over y, x), col: 8 (over z, core).
Axes of the slice: x: 4, y: 4, z: 4, core: 2. Of those that a mesh axis runs over, the one named last changes fastest.
Arguments:
- snapshots: float32 [65536, 2048], P(('row', 'col')), may hold values from -6 to 6
- district: int32 [65536], P(('row', 'col')), may hold values from 0 to 255, never falling along the last dimension, each value on 1 to 1024 neighbouring positions
- target: int32 [65536], replicated, may hold values from 0 to 65535, as said below
Outputs:
- coefficients: float32 [512, 2048], P(None, 'col')
- remainder: float32 [65536, 2048], P('row', 'col')
Inputs may be any that keep to these rules, and one draw needn't show every extreme that they name: A permutation of the storage rows; each aligned block of 512 nodes has exactly 512 / 16 nodes whose target lies in each aligned block of 4096 storage rows. `district`: districts never fall along the nodes, and each holds at most 1024 nodes.
All inputs are finite; a program needn't handle non-finite values.
Results may differ from a plain program's by a relative error of at most 0.0001.
Values sent between devices are 32-bit elements; how exact they have to be, the bound alone decides.
A program may use at most 128 MiB of HBM per device.

v0:
```python
import jax
import jax.numpy as jnp
from jax import lax
from jax.sharding import PartitionSpec as P

NB = 256
DIST_MEAN = 256
HIGH = lax.Precision.HIGHEST


def from_root(value, axis, source):
    kept = jnp.where(lax.axis_index(axis) == source, value, 0).astype(value.dtype)
    return lax.psum(kept, axis)


def orthonormal(panel, gram):
    lower = jnp.linalg.cholesky(gram)
    inverse = jax.scipy.linalg.solve_triangular(
        lower, jnp.eye(gram.shape[0], dtype=gram.dtype), lower=True
    )
    return jnp.dot(panel, inverse.T, precision=HIGH)


def gram_of(panel):
    return jnp.dot(panel.T, panel, precision=HIGH)


def body(snapshots, district, target):
    n_row = lax.axis_size("row")
    n_col = lax.axis_size("col")
    nodes_dev, snaps = snapshots.shape
    nodes = target.shape[0]
    groups = nodes // DIST_MEAN
    labels = jnp.arange(groups, dtype=jnp.int32)
    member = (district[:, None] == labels[None, :]).astype(jnp.float32)
    counts = lax.psum(jnp.sum(member, axis=0), ("row", "col"))
    scale = jnp.sqrt(DIST_MEAN / jnp.maximum(counts, 1.0))
    weight = jnp.dot(member, scale, precision=HIGH)
    weighted = snapshots * weight[:, None]
    local_rows = nodes // n_row
    per_owner = nodes_dev // n_row
    width = snaps // n_col
    source = lax.axis_index(("row", "col"))
    mine = lax.dynamic_slice_in_dim(target, source * nodes_dev, nodes_dev)
    owner = mine // local_rows
    order = jnp.argsort(owner * nodes_dev + jnp.arange(nodes_dev, dtype=jnp.int32))
    sorted_rows = weighted[order]
    shaped = sorted_rows.reshape(n_row, per_owner, width // NB, n_col, NB)
    shaped = shaped.transpose(0, 3, 1, 2, 4).reshape(n_row, n_col, per_owner, width)
    moved = lax.all_to_all(
        shaped.reshape(n_row * n_col, per_owner, width),
        ("row", "col"),
        split_axis=0,
        concat_axis=0,
        tiled=True,
    )
    arrived = moved.reshape(n_row * n_col * per_owner, width)
    my_row = lax.axis_index("row")
    chosen = jnp.nonzero(target // local_rows == my_row, size=local_rows)[0]
    placing = target[chosen] % local_rows
    inverse = (
        jnp.zeros((local_rows,), jnp.int32).at[placing].set(jnp.arange(local_rows, dtype=jnp.int32))
    )
    block = arrived[inverse]
    stacked = []
    for index in range(2):
        first = index // n_col * NB
        panel = block
        gram = lax.psum(gram_of(panel), "row")
        basis = from_root(orthonormal(panel, gram), "col", index % n_col)
        projection = lax.psum(jnp.dot(basis.T, block, precision=HIGH), "row")
        block = block - jnp.dot(basis, projection, precision=HIGH)
        stacked.append(projection)
    return (jnp.concatenate(stacked, axis=0), block)


def solution(mesh):
    in_specs = (P(("row", "col"), None), P(("row", "col")), P())
    out_specs = (P(None, "col"), P("row", "col"))
    return jax.shard_map(body, mesh=mesh, in_specs=in_specs, out_specs=out_specs, check_vma=False)
```

profile of v0, /device:TPU:0, one launch (start us, length us, event | category | flops | bytes accessed | tf_op | source)
XLA Modules:
  0.0 1310.8 jit_solution(6391460466063920243)
XLA Ops:
  12.6 68.2 %psum.49 = f32[256]{0:T(256)S(1)} all-reduce(f32[256]{0:T(256)S(1)} %convert_reduce_fusion), channel_id=1, replica_groups=mesh['row'=16,'col'=8] {'row','col'}, use_global_device_ids=true, to_apply=%region_1.0 | all-reduce | flops 256 | bytes 2048 | tf_op jit(solution)/shard_map/psum | solution.py:36
  81.8 4.6 broadcast_multiply_fusion
  86.4 7.6 gather_fusion
  101.4 6.0 all-to-all-start
  109.9 452.2 %scatter_custom_fusion = s32[4096]{0:T(1024)S(1)} fusion(s32[65536]{0:T(1024)S(1)} %bitcast.103, s32[65536]{0:T(1024)S(1)} %ne.84, s32[]{:T(128)} %copy.53), kind=kCustom, calls=%fused_computation.94 | custom fusion | flops 65536 | bytes 16388 | tf_op jit(solution)/shard_map/scatter-add | solution.py:59
  563.4 23.0 %gather_fusion.1 = s32[4096]{0:T(1024)S(1)} fusion(s32[65536]{0:T(1024)S(1)} %copy-done, s32[4096]{0:T(1024)S(1)} %broadcast_clamp_fusion), kind=kCustom, calls=%fused_computation.1 | custom fusion | bytes 49152 | tf_op jit(solution)/shard_map/gather | solution.py:60
  586.6 15.5 %scatter_custom_fusion.1 = s32[4096]{0:T(1024)S(1)} fusion(s32[4096]{0:T(1024)S(1)} %bitcast.108, s32[4096]{0:T(1024)S(1)} %iota.77, s32[]{:T(128)} %copy.53), kind=kCustom, calls=%fused_computation.92 | custom fusion | bytes 16388 | tf_op jit(solution)/shard_map/scatter | solution.py:62
  602.1 18.3 %gather_fusion.2 = f32[4096,256]{1,0:T(8,128)} fusion(f32[4096,256]{1,0:T(8,128)} %bitcast.4, s32[4096]{0:T(1024)S(1)} %fusion.28), kind=kCustom, calls=%fused_computation.2 | custom fusion | bytes 8404992 | tf_op jit(solution)/shard_map/gather | solution.py:64
  620.4 10.9 fusion.44
  631.7 84.8 %all-reduce.9.cloned.1.call-done = f32[256,256]{0,1:T(8,128)} async-done(((f32[256,256]{0,1:T(8,128)}), f32[256,256]{0,1:T(8,128)}) %all-reduce.9.cloned.1.call-update) | async-done | bytes 262160 | tf_op jit(solution)/shard_map/psum | solution.py:69
  718.6 11.7 cholesky.130
  730.4 9.8 custom-call.13
  740.7 11.7 cholesky.147
  754.6 4.5 while.4
  759.1 19.7 %custom-call.14 = f32[2,128,128]{1,2,0:T(8,128)S(1)} custom-call(f32[2,128,128]{2,1,0:T(8,128)S(1)} %get-tuple-element.20), custom_call_target="InvertDiagBlocksLowerTriangular" | custom-call | tf_op jit(solution)/shard_map/jit(_solve_triangular)/triangular_solve | solution.py:18
  779.7 7.6 convolution_select_fusion.1
  787.4 72.5 %all-reduce.11.cloned.1.call-done = f32[4096,256]{1,0:T(8,128)} async-done(((f32[4096,256]{1,0:T(8,128)}), f32[4096,256]{1,0:T(8,128)}) %all-reduce.11.cloned.1.call-update) | async-done | bytes 4194320 | tf_op jit(solution)/shard_map/psum | solution.py:13
  859.9 10.9 fusion.45
  871.1 83.8 %all-reduce.13.cloned.1.call-done = f32[256,256]{1,0:T(8,128)} async-done(((f32[256,256]{1,0:T(8,128)}), f32[256,256]{1,0:T(8,128)}) %all-reduce.13.cloned.1.call-update) | async-done | bytes 262160 | tf_op jit(solution)/shard_map/psum | solution.py:71
  954.9 7.0 convolution_subtract_fusion.1
  963.9 7.4 fusion.46
  971.6 83.3 %all-reduce.15.cloned.1.call-done = f32[256,256]{0,1:T(8,128)} async-done(((f32[256,256]{0,1:T(8,128)}), f32[256,256]{0,1:T(8,128)}) %all-reduce.15.cloned.1.call-update) | async-done | bytes 262160 | tf_op jit(solution)/shard_map/psum | solution.py:69
  1057.0 11.7 cholesky.164
  1068.8 9.8 custom-call.15
  1079.1 11.7 cholesky.181
  1093.6 4.5 while.5
  1098.1 19.7 %custom-call.16 = f32[2,128,128]{1,2,0:T(8,128)S(1)} custom-call(f32[2,128,128]{2,1,0:T(8,128)S(1)} %get-tuple-element.21), custom_call_target="InvertDiagBlocksLowerTriangular" | custom-call | tf_op jit(solution)/shard_map/jit(_solve_triangular)/triangular_solve | solution.py:18
  1118.7 7.6 convolution_select_fusion
  1126.6 72.4 %all-reduce.17.cloned.1.call-done = f32[4096,256]{1,0:T(8,128)} async-done(((f32[4096,256]{1,0:T(8,128)}), f32[4096,256]{1,0:T(8,128)}) %all-reduce.17.cloned.1.call-update) | async-done | bytes 4194320 | tf_op jit(solution)/shard_map/psum | solution.py:13
  1198.9 10.9 fusion.47
  1209.9 84.0 %all-reduce.19.cloned.1.call-done = f32[256,256]{1,0:T(8,128)} async-done(((f32[256,256]{1,0:T(8,128)}), f32[256,256]{1,0:T(8,128)}) %all-reduce.19.cloned.1.call-update) | async-done | bytes 262160 | tf_op jit(solution)/shard_map/psum | solution.py:71
  1293.9 9.0 convolution_subtract_fusion
  (101 shorter events, 39.1 us)
Async XLA Ops:
  101.4 6.0 copy-start
  101.4 500.7 %all-to-all-start = ((f32[128,32,256]{2,1,0:T(8,128)}), f32[128,32,256]{2,1,0:T(8,128)}, u32[]{:S(2)}, u32[]{:S(2)}) async-start(f32[128,32,256]{2,1,0:T(8,128)} %bitcast.100), calls=%async_computation | async-start | bytes 8388608 | tf_op jit(solution)/shard_map/all_to_all | solution.py:50
  107.4 609.1 %all-reduce.9.cloned.1.call-start = ((), (), s32[]{:S(2)}) async-start(), calls=%async_computation.1 | async-start | bytes 524288 | tf_op jit(solution)/shard_map/psum | solution.py:69
  631.4 228.6 %all-reduce.11.cloned.1.call-start = ((), (), s32[]{:S(2)}) async-start(), calls=%async_computation.2 | async-start | bytes 8388608 | tf_op jit(solution)/shard_map/psum | solution.py:13
  787.4 167.6 %all-reduce.13.cloned.1.call-start = ((), (), s32[]{:S(2)}) async-start(), calls=%async_computation.3 | async-start | bytes 524288 | tf_op jit(solution)/shard_map/psum | solution.py:71
  870.9 184.1 %all-reduce.15.cloned.1.call-start = ((), (), s32[]{:S(2)}) async-start(), calls=%async_computation.4 | async-start | bytes 524288 | tf_op jit(solution)/shard_map/psum | solution.py:69
  961.9 2.0 copy-start.1
  971.4 227.5 %all-reduce.17.cloned.1.call-start = ((), (), s32[]{:S(2)}) async-start(), calls=%async_computation.5 | async-start | bytes 8388608 | tf_op jit(solution)/shard_map/psum | solution.py:13
  1126.4 167.6 %all-reduce.19.cloned.1.call-start = ((), (), s32[]{:S(2)}) async-start(), calls=%async_computation.6 | async-start | bytes 524288 | tf_op jit(solution)/shard_map/psum | solution.py:71
  1209.9 93.1 %copy-start.2 = (f32[256,256]{1,0:T(8,128)S(1)}, f32[256,256]{1,0:T(8,128)}, u32[]{:S(2)}) copy-start(f32[256,256]{1,0:T(8,128)} %all-reduce.13.cloned.1.call-done) | copy-start | bytes 786436
  1293.9 9.0 copy-start.3
Sparse Core Ops, SparseCore 0:
  631.5 84.9 all-reduce.8
  787.5 72.4 all-reduce.10
  871.0 83.8 all-reduce.12
  971.5 83.3 all-reduce.14
  1126.5 72.4 all-reduce.16
  1210.0 83.8 all-reduce.18
where the time goes:
time: 1320 us; the launch traced here: 1310 us
  other arithmetic  576 us (44%)
  waiting for transfers between devices  481 us (36%)
  local copies, waits for them, and re-layouts  85.1 us (6%)
  matrix products  75.2 us (6%)
  blocking collectives  68.2 us (5%)
  between operations  17.4 us (1%)
    scatter-add x1, other arithmetic, body(): chosen = jnp.nonzero(target // local_rows == my_row, size=local_rows)[0]  452 us
    psum x2, waiting for transfers between devices, body(): gram = lax.psum(gram_of(panel), 'row')  168 us
    psum x2, waiting for transfers between devices, body(): projection = lax.psum(jnp.dot(basis.T, block, precision=HIGH), 'row')  168 us
    psum x2, waiting for transfers between devices, from_root(): return lax.psum(kept, axis)  145 us
    another operation x13, other arithmetic, orthonormal(): lower = jnp.linalg.cholesky(gram)  68.7 us
    psum x1, blocking collectives, body(): counts = lax.psum(jnp.sum(member, axis=0), ('row', 'col'))  68.2 us
    another operation x5, other arithmetic, orthonormal(): jax.scipy.linalg.solve_triangular(lower, jnp.eye(gram.shape[0], dtype=gra...  39.4 us
  transfers between devices with their start and end apart: 7, of which 6 were waited for; matrix products, arithmetic and copies ran while one was open for 38% of the time, Pallas kernels for 0%

commit v1 on v0

--- a/solution.py
+++ b/solution.py
@@ -68,7 +68,7 @@
         panel = block
         gram = lax.psum(gram_of(panel), "row")
         basis = from_root(orthonormal(panel, gram), "col", index % n_col)
-        projection = lax.psum(jnp.dot(basis.T, block, precision=HIGH), "row")
+        projection = jnp.sum(lax.all_gather(jnp.dot(basis.T, block, precision=HIGH), "row"), axis=0)
         block = block - jnp.dot(basis, projection, precision=HIGH)
         stacked.append(projection)
     return (jnp.concatenate(stacked, axis=0), block)

time: 1320 us -> 1260 us (0.955)
  waiting for transfers between devices: 481 us -> 416 us
    psum x2 -> x0, waiting for transfers between devices: 168 us -> none  [body(): projection = lax.psum(jnp.dot(basis.T, block, precision=HIGH), 'row')]
    all_gather x0 -> x2, waiting for transfers between devices: none -> 103 us  [body(): lax.all_gather(jnp.dot(basis.T, block, precision=HIGH), 'row')]
  transfers between devices with their start and end apart: 7 -> 7, of which waited for: 6 -> 6; matrix products, arithmetic and copies ran while one was open for 38% -> 40% of each run, Pallas kernels for 0% -> 0%
where the time goes in v1:
time: 1260 us; the launch traced here: 1250 us
  other arithmetic  581 us (46%)
  waiting for transfers between devices  416 us (33%)
  local copies, waits for them, and re-layouts  85.1 us (7%)
  matrix products  74.9 us (6%)
  blocking collectives  68.2 us (5%)
  between operations  17.4 us (1%)
    scatter-add x1, other arithmetic, body(): chosen = jnp.nonzero(target // local_rows == my_row, size=local_rows)[0]  452 us
    psum x2, waiting for transfers between devices, body(): gram = lax.psum(gram_of(panel), 'row')  168 us
    psum x2, waiting for transfers between devices, from_root(): return lax.psum(kept, axis)  145 us
    all_gather x2, waiting for transfers between devices, body(): lax.all_gather(jnp.dot(basis.T, block, precision=HIGH), 'row')  103 us
    another operation x13, other arithmetic, orthonormal(): lower = jnp.linalg.cholesky(gram)  68.7 us
    psum x1, blocking collectives, body(): counts = lax.psum(jnp.sum(member, axis=0), ('row', 'col'))  68.2 us
    another operation x5, other arithmetic, orthonormal(): jax.scipy.linalg.solve_triangular(lower, jnp.eye(gram.shape[0], dtype=gra...  39.4 us
  transfers between devices with their start and end apart: 7, of which 6 were waited for; matrix products, arithmetic and copies ran while one was open for 40% of the time, Pallas kernels for 0%

profile of v1, /device:TPU:0, one launch (start us, length us, event | category | flops | bytes accessed | tf_op | source)
XLA Modules:
  0.0 1250.6 jit_solution(17631276507633062015)
XLA Ops:
  12.6 68.2 %psum.35 = f32[256]{0:T(256)S(1)} all-reduce(f32[256]{0:T(256)S(1)} %convert_reduce_fusion), channel_id=1, replica_groups=mesh['row'=16,'col'=8] {'row','col'}, use_global_device_ids=true, to_apply=%region_1.0 | all-reduce | flops 256 | bytes 2048 | tf_op jit(solution)/shard_map/psum | solution.py:36
  81.8 4.6 broadcast_multiply_fusion
  86.4 7.6 gather_fusion
  101.4 6.0 all-to-all-start
  109.9 452.2 %scatter_custom_fusion = s32[4096]{0:T(1024)S(1)} fusion(s32[65536]{0:T(1024)S(1)} %bitcast.107, s32[65536]{0:T(1024)S(1)} %ne.84, s32[]{:T(128)} %copy.53), kind=kCustom, calls=%fused_computation.94 | custom fusion | flops 65536 | bytes 16388 | tf_op jit(solution)/shard_map/scatter-add | solution.py:59
  563.4 23.0 %gather_fusion.1 = s32[4096]{0:T(1024)S(1)} fusion(s32[65536]{0:T(1024)S(1)} %copy-done, s32[4096]{0:T(1024)S(1)} %broadcast_clamp_fusion), kind=kCustom, calls=%fused_computation.1 | custom fusion | bytes 49152 | tf_op jit(solution)/shard_map/gather | solution.py:60
  586.6 15.5 %scatter_custom_fusion.1 = s32[4096]{0:T(1024)S(1)} fusion(s32[4096]{0:T(1024)S(1)} %bitcast.112, s32[4096]{0:T(1024)S(1)} %iota.77, s32[]{:T(128)} %copy.53), kind=kCustom, calls=%fused_computation.92 | custom fusion | bytes 16388 | tf_op jit(solution)/shard_map/scatter | solution.py:62
  602.1 18.3 %gather_fusion.2 = f32[4096,256]{1,0:T(8,128)} fusion(f32[4096,256]{1,0:T(8,128)} %bitcast.4, s32[4096]{0:T(1024)S(1)} %fusion.28), kind=kCustom, calls=%fused_computation.2 | custom fusion | bytes 8404992 | tf_op jit(solution)/shard_map/gather | solution.py:64
  620.4 10.9 fusion.44
  631.7 84.8 %all-reduce.7.cloned.1.call-done = f32[256,256]{0,1:T(8,128)} async-done(((f32[256,256]{0,1:T(8,128)}), f32[256,256]{0,1:T(8,128)}) %all-reduce.7.cloned.1.call-update) | async-done | bytes 262160 | tf_op jit(solution)/shard_map/psum | solution.py:69
  718.6 11.7 cholesky.130
  730.4 9.8 custom-call.13
  740.7 11.7 cholesky.147
  754.6 4.5 while.4
  759.1 19.7 %custom-call.14 = f32[2,128,128]{1,2,0:T(8,128)S(1)} custom-call(f32[2,128,128]{2,1,0:T(8,128)S(1)} %get-tuple-element.20), custom_call_target="InvertDiagBlocksLowerTriangular" | custom-call | tf_op jit(solution)/shard_map/jit(_solve_triangular)/triangular_solve | solution.py:18
  779.7 7.6 convolution_select_fusion.1
  787.4 72.5 %all-reduce.9.cloned.1.call-done = f32[4096,256]{1,0:T(8,128)} async-done(((f32[4096,256]{1,0:T(8,128)}), f32[4096,256]{1,0:T(8,128)}) %all-reduce.9.cloned.1.call-update) | async-done | bytes 4194320 | tf_op jit(solution)/shard_map/psum | solution.py:13
  859.9 10.9 fusion.45
  871.1 51.2 %all-gather.5.cloned.1.call-done = f32[4096,256]{1,0:T(8,128)} async-done(((f32[256,256]{1,0:T(8,128)}), f32[4096,256]{1,0:T(8,128)}) %all-gather.5.cloned.1.call-update) | async-done | bytes 4194320 | tf_op jit(solution)/shard_map/all_gather | solution.py:71
  924.8 6.9 convolution_subtract_fusion.1
  933.7 7.4 fusion.46
  941.4 83.6 %all-reduce.11.cloned.1.call-done = f32[256,256]{0,1:T(8,128)} async-done(((f32[256,256]{0,1:T(8,128)}), f32[256,256]{0,1:T(8,128)}) %all-reduce.11.cloned.1.call-update) | async-done | bytes 262160 | tf_op jit(solution)/shard_map/psum | solution.py:69
  1027.1 11.7 cholesky.164
  1038.9 9.8 custom-call.15
  1049.2 11.7 cholesky.181
  1063.7 4.5 while.5
  1068.2 19.7 %custom-call.16 = f32[2,128,128]{1,2,0:T(8,128)S(1)} custom-call(f32[2,128,128]{2,1,0:T(8,128)S(1)} %get-tuple-element.21), custom_call_target="InvertDiagBlocksLowerTriangular" | custom-call | tf_op jit(solution)/shard_map/jit(_solve_triangular)/triangular_solve | solution.py:18
  1088.8 7.6 convolution_select_fusion
  1096.6 72.3 %all-reduce.13.cloned.1.call-done = f32[4096,256]{1,0:T(8,128)} async-done(((f32[4096,256]{1,0:T(8,128)}), f32[4096,256]{1,0:T(8,128)}) %all-reduce.13.cloned.1.call-update) | async-done | bytes 4194320 | tf_op jit(solution)/shard_map/psum | solution.py:13
  1169.0 10.9 fusion.47
  1179.9 51.4 %all-gather.7.cloned.1.call-done = f32[4096,256]{1,0:T(8,128)} async-done(((f32[256,256]{1,0:T(8,128)}), f32[4096,256]{1,0:T(8,128)}) %all-gather.7.cloned.1.call-update) | async-done | bytes 4194320 | tf_op jit(solution)/shard_map/all_gather | solution.py:71
  1234.7 8.9 convolution_subtract_fusion
  (99 shorter events, 44.0 us)
Async XLA Ops:
  101.4 6.0 copy-start
  101.4 500.7 %all-to-all-start = ((f32[128,32,256]{2,1,0:T(8,128)}), f32[128,32,256]{2,1,0:T(8,128)}, u32[]{:S(2)}, u32[]{:S(2)}) async-start(f32[128,32,256]{2,1,0:T(8,128)} %bitcast.102), calls=%async_computation | async-start | bytes 8388608 | tf_op jit(solution)/shard_map/all_to_all | solution.py:50
  107.4 609.1 %all-reduce.7.cloned.1.call-start = ((), (), s32[]{:S(2)}) async-start(), calls=%async_computation.1 | async-start | bytes 524288 | tf_op jit(solution)/shard_map/psum | solution.py:69
  631.4 228.5 %all-reduce.9.cloned.1.call-start = ((), (), s32[]{:S(2)}) async-start(), calls=%async_computation.2 | async-start | bytes 8388608 | tf_op jit(solution)/shard_map/psum | solution.py:13
  787.3 135.0 %all-gather.5.cloned.1.call-start = ((), (), s32[]{:S(2)}) async-start(), calls=%async_computation.5 | async-start | bytes 4456448 | tf_op jit(solution)/shard_map/all_gather | solution.py:71
  870.8 154.2 %all-reduce.11.cloned.1.call-start = ((), (), s32[]{:S(2)}) async-start(), calls=%async_computation.3 | async-start | bytes 524288 | tf_op jit(solution)/shard_map/psum | solution.py:69
  931.7 2.0 copy-start.1
  941.1 227.8 %all-reduce.13.cloned.1.call-start = ((), (), s32[]{:S(2)}) async-start(), calls=%async_computation.4 | async-start | bytes 8388608 | tf_op jit(solution)/shard_map/psum | solution.py:13
  1096.4 134.9 %all-gather.7.cloned.1.call-start = ((), (), s32[]{:S(2)}) async-start(), calls=%async_computation.6 | async-start | bytes 4456448 | tf_op jit(solution)/shard_map/all_gather | solution.py:71
Sparse Core Ops, SparseCore 0:
  631.5 84.9 all-reduce.6
  787.5 72.3 all-reduce.8
  871.0 51.2 all-gather.4
  941.3 83.6 all-reduce.10
  1096.5 72.3 all-reduce.12
  1180.0 51.2 all-gather.6
